TPU v7x, 512 devices: a whole 4x4x16 slice. The times are simulated.
512 devices in a mesh: dp: 8 (over y, x_hi), context: 64 (over x_lo, z, core).
Axes of the slice: x: 4 (x_hi: 2, x_lo: 2; x = x_hi * 2 + x_lo), y: 4, z: 16, core: 2. Of those that a mesh axis runs over, the one named last changes fastest.
Arguments:
- codes: int32 [8, 65536], P('dp', 'context'), may hold values from 0 to 3
- variant_pos: int32 [8, 64], P('dp'), may hold values from 0 to 65535
- variant_shift: int32 [8, 64], P('dp'), may hold values from 1 to 3
- stem_weight: float32 [15, 4, 384], replicated, may hold values from -1.5 to 1.5
- conv_weight: bfloat16 [5, 384, 384], replicated, may hold values from -0.125 to 0.125
- cotangent: bfloat16 [8, 32768, 384], P('dp', 'context'), may hold values from -6 to 6
Outputs:
- features: bfloat16 [8, 32768, 384], P('dp', 'context')
- d_pooled: bfloat16 [8, 32768, 384], P('dp', 'context')
- conv_grad: float32 [5, 384, 384], replicated
- stem_grad: float32 [15, 4, 384], replicated
All inputs are finite; a program needn't handle non-finite values.
Results may differ from a plain program's by a relative error of at most 0.009.
Values may be sent and summed in bfloat16 or wider, within the bound.
A program may use at most 64 MiB of HBM per device.

v0:
```python
import math
import jax
import jax.numpy as jnp
from jax import lax
from jax.sharding import PartitionSpec as P

root_scale = math.sqrt(2.0 / math.pi)
cubic = 0.044715


def with_halo(block, sides, width):
    for axis, dim in sides:
        count = lax.axis_size(axis)
        forward = [(i, i + 1) for i in range(count - 1)]
        backward = [(target, source) for source, target in forward]
        low = lax.ppermute(
            lax.slice_in_dim(block, block.shape[dim] - width, None, axis=dim), axis, forward
        )
        high = lax.ppermute(lax.slice_in_dim(block, 0, width, axis=dim), axis, backward)
        block = jnp.concatenate([low, block, high], axis=dim)
    return block


def gelu_tanh(value):
    return 0.5 * value * (1.0 + jnp.tanh(root_scale * (value + cubic * value * value * value)))


def gelu_slope(value):
    inner = jnp.tanh(root_scale * (value + cubic * value * value * value))
    return 0.5 * (1.0 + inner) + 0.5 * value * (1.0 - inner * inner) * root_scale * (
        1.0 + 3.0 * cubic * value * value
    )


def per_device(codes, variant_pos, variant_shift, stem_weight, conv_weight, cotangent):
    length = codes.shape[1]
    half_rows = length // 2
    width = stem_weight.shape[2]
    first_base = lax.axis_index("context") * length
    places = first_base + jnp.arange(length, dtype=jnp.int32)
    matches = (variant_pos[:, None, :] == places[None, :, None]).astype(jnp.int32)
    shifts = jnp.sum(matches * variant_shift[:, None, :], axis=2)
    mutated = (codes + shifts) % 4 + 1
    extended = with_halo(mutated, (("context", 1),), 7)
    onehot = (extended[:, :, None] == jnp.arange(1, 5, dtype=jnp.int32)[None, None, :]).astype(
        jnp.float32
    )
    windows = jnp.concatenate([onehot[:, k : k + length] for k in range(15)], axis=2)
    flat_stem = stem_weight.reshape(60, width)
    stem = jnp.einsum(
        "blk,kc->blc",
        windows,
        flat_stem,
        precision=lax.Precision.HIGHEST,
        preferred_element_type=jnp.float32,
    )
    active = gelu_tanh(stem)
    pooled = (0.5 * (active[:, 0::2] + active[:, 1::2])).astype(jnp.bfloat16)
    pooled_f = pooled.astype(jnp.float32)
    gated = gelu_tanh(pooled_f).astype(jnp.bfloat16)
    gated_ext = with_halo(gated, (("context", 1),), 2)
    cot_ext = with_halo(cotangent, (("context", 1),), 2)
    conv_out = jnp.zeros((gated.shape[0], half_rows, width), jnp.float32)
    back = jnp.zeros((gated.shape[0], half_rows, width), jnp.float32)
    for offset in range(5):
        conv_out = conv_out + jnp.einsum(
            "brc,cd->brd",
            gated_ext[:, offset : offset + half_rows],
            conv_weight[offset],
            preferred_element_type=jnp.float32,
        )
        back = back + jnp.einsum(
            "brd,cd->brc",
            cot_ext[:, 4 - offset : 4 - offset + half_rows],
            conv_weight[offset],
            preferred_element_type=jnp.float32,
        )
    features = (pooled_f + conv_out).astype(jnp.bfloat16)
    dpool = cotangent.astype(jnp.float32) + back * gelu_slope(pooled_f)
    d_pooled = dpool.astype(jnp.bfloat16)
    tap_grads = jnp.stack(
        [
            jnp.einsum(
                "brc,brd->cd",
                gated_ext[:, offset : offset + half_rows],
                cotangent,
                preferred_element_type=jnp.float32,
            )
            for offset in range(5)
        ]
    )
    dstem = 0.5 * jnp.repeat(dpool, 2, axis=1) * gelu_slope(stem)
    stem_part = jnp.einsum(
        "blk,blc->kc",
        windows,
        dstem,
        precision=lax.Precision.HIGHEST,
        preferred_element_type=jnp.float32,
    )
    stem_grad = lax.psum(stem_part, ("dp", "context")).reshape(15, 4, width)
    conv_grad = lax.psum(tap_grads, ("dp", "context"))
    return (features, d_pooled, conv_grad, stem_grad)


def solution(mesh):
    placed = (P("dp", "context"), P("dp", None), P("dp", None), P(), P(), P("dp", "context", None))
    return jax.shard_map(
        per_device,
        mesh=mesh,
        in_specs=placed,
        out_specs=(P("dp", "context", None), P("dp", "context", None), P(), P()),
        check_vma=False,
    )
```

profile of v0, /device:TPU:2, one launch (start us, length us, event | category | flops | bytes accessed | tf_op | source)
XLA Modules:
  0.0 567.2 jit_solution(724238133295681119)
XLA Ops:
  8.8 10.8 %collective-permute-start.1 = (s32[1,7]{1,0:T(1,128)S(1)}, s32[1,7]{1,0:T(1,128)S(1)}, u32[]{:S(2)}, u32[]{:S(2)}) collective-permute-start(s32[1,7]{1,0:T(1,128)S(1)} %get-tuple-element.14), channel_id=1, source_target_pairs={{1,0},{2,1},{3,2},{4,3},{5,4},{6,5},{7,6},{8,7},{9,8},{10,9},{11,1... | collective-permute-start | bytes 92 | tf_op jit(solution)/shard_map/ppermute | solution.py:19
  19.6 1.9 collective-permute-start
  21.5 1.3 fusion.112
  22.8 1.9 collective-permute-start.5
  24.7 5.8 %collective-permute-start.4 = (bf16[1,2,384]{2,1,0:T(2,128)(2,1)}, bf16[1,2,384]{2,1,0:T(2,128)(2,1)S(1)}, u32[]{:S(2)}, u32[]{:S(2)}) collective-permute-start(bf16[1,2,384]{2,1,0:T(2,128)(2,1)} %get-tuple-element.11), channel_id=1, source_target_pairs={{1,0},{2,1},{3,2},{4,3},{5,4},{6,5},{7,6},{8,7},{9,8},{10,9},{11,1... | collective-permute-start | bytes 4616 | tf_op jit(solution)/shard_map/ppermute | solution.py:19
  30.5 1.8 constant_dynamic-update-slice_fusion.16
  33.2 2.4 fusion.59
  37.4 1.5 fusion.75
  39.3 2.8 slice.143
  42.1 2.8 slice.142
  44.9 1.9 fusion.29
  47.4 2.4 collective-permute-start.3
  49.8 2.1 collective-permute-start.2
  53.8 1.6 multiply_bitcast_fusion.1
  55.9 2.2 mul.172
  58.2 3.6 fusion.6
  62.4 1.2 fusion.25
  63.7 1.2 fusion.24
  64.9 1.3 fusion.23
  66.2 1.2 fusion.22
  67.4 1.2 fusion.21
  68.7 1.3 copy-done.1
  72.8 483.2 %all-reduce.3.cloned.1.call-done = (f32[5,384,384]{2,1,0:T(8,128)}, f32[15,4,384]{2,1,0:T(4,128)}) async-done(((f32[5,384,384]{2,1,0:T(8,128)}, f32[15,4,384]{2,1,0:T(4,128)}), (f32[5,384,384]{2,1,0:T(8,128)}, f32[15,4,384]{2,1,0:T(4,128)})) %all-reduce.3.cloned.1.call-update) | async-done | bytes 3041296 | tf_op jit(solution)/shard_map/psum | solution.py:101
  556.0 3.7 copy.40
  (65 shorter events, 11.8 us)
Async XLA Ops:
  7.2 548.9 %all-reduce.3.cloned.1.call-start = ((), (), s32[]{:S(2)}) async-start(), calls=%async_computation | async-start | bytes 6082560 | tf_op jit(solution)/shard_map/psum | solution.py:101
  8.8 26.8 %collective-permute-start.1 = (s32[1,7]{1,0:T(1,128)S(1)}, s32[1,7]{1,0:T(1,128)S(1)}, u32[]{:S(2)}, u32[]{:S(2)}) collective-permute-start(s32[1,7]{1,0:T(1,128)S(1)} %get-tuple-element.14), channel_id=1, source_target_pairs={{1,0},{2,1},{3,2},{4,3},{5,4},{6,5},{7,6},{8,7},{9,8},{10,9},{11,1... | collective-permute-start | bytes 92 | tf_op jit(solution)/shard_map/ppermute | solution.py:19
  19.6 16.0 %collective-permute-start = (s32[1,7]{1,0:T(1,128)S(1)}, s32[1,7]{1,0:T(1,128)S(1)}, u32[]{:S(2)}, u32[]{:S(2)}) collective-permute-start(s32[1,7]{1,0:T(1,128)S(1)} %get-tuple-element.15), channel_id=1, source_target_pairs={{0,1},{1,2},{2,3},{3,4},{4,5},{5,6},{6,7},{7,8},{8,9},{9,10},{10,1... | collective-permute-start | bytes 92 | tf_op jit(solution)/shard_map/ppermute | solution.py:16
  22.8 30.0 %collective-permute-start.5 = (bf16[1,2,384]{2,1,0:T(2,128)(2,1)}, bf16[1,2,384]{2,1,0:T(2,128)(2,1)S(1)}, u32[]{:S(2)}, u32[]{:S(2)}) collective-permute-start(bf16[1,2,384]{2,1,0:T(2,128)(2,1)} %get-tuple-element.10), channel_id=1, source_target_pairs={{0,1},{1,2},{2,3},{3,4},{4,5},{5,6},{6,7},{7,8},{8,9},{9,10},{10,1... | collective-permute-start | bytes 4616 | tf_op jit(solution)/shard_map/ppermute | solution.py:16
  24.7 27.2 %collective-permute-start.4 = (bf16[1,2,384]{2,1,0:T(2,128)(2,1)}, bf16[1,2,384]{2,1,0:T(2,128)(2,1)S(1)}, u32[]{:S(2)}, u32[]{:S(2)}) collective-permute-start(bf16[1,2,384]{2,1,0:T(2,128)(2,1)} %get-tuple-element.11), channel_id=1, source_target_pairs={{1,0},{2,1},{3,2},{4,3},{5,4},{6,5},{7,6},{8,7},{9,8},{10,9},{11,1... | collective-permute-start | bytes 4616 | tf_op jit(solution)/shard_map/ppermute | solution.py:19
  37.4 1.9 copy-start.8
  44.8 7.1 %copy-start.4 = (bf16[1,514,384]{2,1,0:T(8,128)(2,1)S(1)}, bf16[1,514,384]{2,1,0:T(8,128)(2,1)}, u32[]{:S(2)}) copy-start(bf16[1,514,384]{2,1,0:T(8,128)(2,1)} %constant_dynamic-update-slice_fusion.16) | copy-start | bytes 1184260
  44.9 7.1 %copy-start = (bf16[5,384,384]{2,1,0:T(8,128)(2,1)S(1)}, bf16[5,384,384]{2,1,0:T(8,128)(2,1)}, u32[]{:S(2)}) copy-start(bf16[5,384,384]{2,1,0:T(8,128)(2,1)} %param.10) | copy-start | bytes 4423684
  44.9 7.5 %copy-start.5 = (f32[512,384]{1,0:T(8,128)S(1)}, f32[512,384]{1,0:T(8,128)}, u32[]{:S(2)}) copy-start(f32[512,384]{1,0:T(8,128)} %fusion.59) | copy-start | bytes 2359300
  46.7 7.1 %copy-start.6 = (bf16[1,512,384]{2,1,0:T(8,128)(2,1)}, bf16[1,512,384]{2,1,0:T(8,128)(2,1)S(1)}, u32[]{:S(2)}) copy-start(bf16[1,512,384]{2,1,0:T(8,128)(2,1)S(1)} %get-tuple-element.7) | copy-start | bytes 1179652
  47.4 18.8 %collective-permute-start.3 = (bf16[1,2,384]{2,1,0:T(2,128)(2,1)}, bf16[1,2,384]{2,1,0:T(2,128)(2,1)S(1)}, u32[]{:S(2)}, u32[]{:S(2)}) collective-permute-start(bf16[1,2,384]{2,1,0:T(2,128)(2,1)} %get-tuple-element.12), channel_id=1, source_target_pairs={{1,0},{2,1},{3,2},{4,3},{5,4},{6,5},{7,6},{8,7},{9,8},{10,9},{11,1... | collective-permute-start | bytes 4616 | tf_op jit(solution)/shard_map/ppermute | solution.py:19
  49.8 12.7 %collective-permute-start.2 = (bf16[1,2,384]{2,1,0:T(2,128)(2,1)}, bf16[1,2,384]{2,1,0:T(2,128)(2,1)S(1)}, u32[]{:S(2)}, u32[]{:S(2)}) collective-permute-start(bf16[1,2,384]{2,1,0:T(2,128)(2,1)} %get-tuple-element.13), channel_id=1, source_target_pairs={{0,1},{1,2},{2,3},{3,4},{4,5},{5,6},{6,7},{7,8},{8,9},{9,10},{10,1... | collective-permute-start | bytes 4616 | tf_op jit(solution)/shard_map/ppermute | solution.py:16
  52.4 1.0 copy-start.2
  58.2 4.3 copy-start.3
  62.4 2.5 copy-start.7
  68.7 1.4 copy-start.1
  556.0 3.7 copy-start.9
Sparse Core Ops, SparseCore 0:
  68.8 487.1 all-reduce.2
where the time goes:
time: 568 us; the launch traced here: 567 us
  waiting for transfers between devices  483 us (85%)
  starting transfers between devices  24.9 us (4%)
  local copies, waits for them, and re-layouts  21.4 us (4%)
  matrix products  19.3 us (3%)
  between operations  14.4 us (3%)
    psum x1, waiting for transfers between devices, per_device(): conv_grad = lax.psum(tap_grads, ('dp', 'context'))  483 us
    ppermute x3, starting transfers between devices, with_halo(): lax.ppermute(lax.slice_in_dim(block, 0, width, axis=dim), axis, backward)  18.9 us
  transfers between devices with their start and end apart: 7, of which 1 were waited for; matrix products, arithmetic and copies ran while one was open for 6% of the time, Pallas kernels for 0%

commit v1 on v0

--- a/solution.py
+++ b/solution.py
@@ -98,7 +98,7 @@
         preferred_element_type=jnp.float32,
     )
     stem_grad = lax.psum(stem_part, ("dp", "context")).reshape(15, 4, width)
-    conv_grad = lax.psum(tap_grads, ("dp", "context"))
+    conv_grad = lax.psum(lax.psum(tap_grads, "dp"), "context")
     return (features, d_pooled, conv_grad, stem_grad)
 
 

time: 568 us -> 1100 us (1.94)
  the two profiles are of different devices: /device:TPU:2 before, /device:TPU:8 now
where the time goes in v1:
time: 1100 us
  waiting for transfers between devices  1030 us (94%)
  matrix products  18.3 us (2%)
  local copies, waits for them, and re-layouts  17.5 us (2%)
  starting transfers between devices  15 us (1%)
  between operations  14.2 us (1%)
    psum x2, waiting for transfers between devices, per_device(): conv_grad = lax.psum(lax.psum(tap_grads, 'dp'), 'context')  576 us
    psum x1, waiting for transfers between devices, per_device(): stem_grad = lax.psum(stem_part, ('dp', 'context')).reshape(15, 4, width)  453 us
  transfers between devices with their start and end apart: 9, of which 4 were waited for; matrix products, arithmetic and copies ran while one was open for 2% of the time, Pallas kernels for 0%

profile of v1, /device:TPU:8, one launch (start us, length us, event | category | flops | bytes accessed | tf_op | source)
XLA Modules:
  0.0 1099.7 jit_solution(9268334845180871248)
XLA Ops:
  8.8 1.3 collective-permute-start.1
  10.1 3.0 collective-permute-start
  15.8 1.5 fusion.75
  17.8 2.8 slice.143
  20.6 2.8 slice.142
  23.3 1.8 fusion.29
  25.1 3.4 collective-permute-start.2
  28.6 1.3 collective-permute-start.3
  29.9 1.2 fusion.25
  31.1 1.2 fusion.24
  32.4 1.3 fusion.23
  33.7 1.2 fusion.22
  34.9 1.2 fusion.21
  37.1 4.5 collective-permute-start.5
  41.6 1.3 collective-permute-start.4
  42.9 1.4 fusion.59
  44.4 1.5 collective-permute-done.4
  47.8 1.6 multiply_bitcast_fusion.1
  50.0 2.2 mul.172
  52.2 3.5 fusion.6
  56.5 141.4 %all-reduce.4.cloned.1.call-done = f32[5,384,384]{2,1,0:T(8,128)} async-done(((f32[5,384,384]{2,1,0:T(8,128)}), f32[5,384,384]{2,1,0:T(8,128)}) %all-reduce.4.cloned.1.call-update) | async-done | bytes 2949136 | tf_op jit(solution)/shard_map/psum | solution.py:101
  200.9 453.0 %all-reduce.8.cloned.1.call-done = f32[15,4,384]{2,1,0:T(4,128)} async-done(((f32[15,4,384]{2,1,0:T(4,128)}), f32[15,4,384]{2,1,0:T(4,128)}) %all-reduce.8.cloned.1.call-update) | async-done | bytes 92176 | tf_op jit(solution)/shard_map/psum | solution.py:100
  653.9 435.0 %all-reduce.6.cloned.1.call-done = f32[5,384,384]{2,1,0:T(8,128)} async-done(((f32[5,384,384]{2,1,0:T(8,128)}), f32[5,384,384]{2,1,0:T(8,128)}) %all-reduce.6.cloned.1.call-update) | async-done | bytes 2949136 | tf_op jit(solution)/shard_map/psum | solution.py:101
  1088.9 3.7 copy.41
  (69 shorter events, 12.4 us)
Async XLA Ops:
  7.2 190.7 %all-reduce.4.cloned.1.call-start = ((), (), s32[]{:S(2)}) async-start(), calls=%async_computation | async-start | bytes 5898240 | tf_op jit(solution)/shard_map/psum | solution.py:101
  8.8 5.3 collective-permute-start.1
  10.1 4.0 collective-permute-start
  15.8 1.9 copy-start.7
  23.3 6.6 copy-start.2
  25.1 7.2 copy-start.4
  25.1 4.7 collective-permute-start.2
  28.6 5.1 collective-permute-start.3
  36.1 6.8 copy-start
  36.2 617.8 %all-reduce.8.cloned.1.call-start = ((), (), s32[]{:S(2)}) async-start(), calls=%async_computation.2 | async-start | bytes 184320 | tf_op jit(solution)/shard_map/psum | solution.py:100
  36.2 8.1 copy-start.3
  37.1 9.8 collective-permute-start.5
  41.6 4.3 collective-permute-start.4
  46.8 1.0 copy-start.5
  55.7 142.2 %copy-start.1 = (bf16[5,384,384]{2,1,0:T(8,128)(2,1)S(1)}, bf16[5,384,384]{2,1,0:T(8,128)(2,1)}, u32[]{:S(2)}) copy-start(bf16[5,384,384]{2,1,0:T(8,128)(2,1)} %param.10) | copy-start | bytes 4423684
  56.4 1032.4 %all-reduce.6.cloned.1.call-start = ((), (), s32[]{:S(2)}) async-start(), calls=%async_computation.1 | async-start | bytes 5898240 | tf_op jit(solution)/shard_map/psum | solution.py:101
  197.9 1.0 copy-start.6
  1088.9 3.7 copy-start.8
Sparse Core Ops, SparseCore 0:
  36.3 161.5 all-reduce.3
  203.9 449.9 all-reduce.7
  656.8 431.9 all-reduce.5
